TPU v7x, 256 devices: a whole 4x4x8 slice. The times are simulated.
256 devices in a mesh: lon: 64 (over z_hi, y, x, core), lat: 4 (over z_lo).
Axes of the slice: x: 4, y: 4, z: 8 (z_hi: 2, z_lo: 4; z = z_hi * 4 + z_lo), core: 2. Of those that a mesh axis runs over, the one named last changes fastest.
Arguments:
- fields: float32 [8, 64, 16, 8192], P(None, None, 'lat', 'lon'), may hold values from -6 to 6
- courant: float32 [2, 64, 16, 8192], P(None, None, 'lat', 'lon'), may hold values from -0.5 to 0.5
- cos_zenith: float32 [16, 8192], P('lat', 'lon'), may hold values from 0.2 to 1
- albedo: float32 [16, 8192], P('lat', 'lon'), may hold values from 0.05 to 0.5
- extinction: float32 [14], replicated, may hold values from 0.05 to 4
- single_albedo: float32 [14], replicated, may hold values from 0.2 to 0.95
- band_weight: float32 [14], replicated, may hold values from 0.02 to 0.14
- sun_order: int32 [16, 64, 128], P('lat', 'lon'), may hold values from 0 to 127, each once within a row
- sun_count: int32 [16, 64], P('lat', 'lon'), may hold values from 0 to 128, as said below
Outputs:
- new_fields: float32 [8, 64, 16, 8192], P(None, None, 'lat', 'lon')
- heating: float32 [64, 16, 8192], P(None, 'lat', 'lon')
Inputs may be any that keep to these rules, and one draw needn't show every extreme that they name: `sun_count`: for every latitude the counts of tiles t and t + 32 sum to 128.
All inputs are finite; a program needn't handle non-finite values.
Results may differ from a plain program's by a relative error of at most 0.00005.
Values sent between devices are 32-bit elements; how exact they have to be, the bound alone decides.
A program may use at most 128 MiB of HBM per device.

v0:
```python
import functools

import jax
import jax.numpy as jnp
from jax import lax
from jax.experimental import pallas as pl
from jax.experimental.pallas import tpu as pltpu
from jax.sharding import PartitionSpec as P

MESH = pl.DeviceIdType.MESH
HALO = 2


def step_kernel(
    dims,
    fields_hbm,
    flat_hbm,
    courant_hbm,
    cosz_ref,
    albedo_ref,
    ext_ref,
    ssa_ref,
    weight_ref,
    order_ref,
    count_ref,
    out_hbm,
    heat_hbm,
    q_buf,
    s_buf,
    o_buf,
    c_east,
    c_west,
    c_north,
    water_buf,
    heat_buf,
    rad_a,
    rad_b,
    rad_c,
    rad_g,
    pack_own,
    pack_send,
    pack_recv,
    own_sem,
    out_sem,
    z1_send,
    z1_recv,
    z2_send,
    z2_recv,
    cn_send,
    cn_recv,
    x_send,
    x_recv,
):
    nf, lev, rows, lanes, bands, n_lat, n_lon = dims
    groups = lev // 8
    pairs = bands // 2
    lat = lax.axis_index("lat")
    lon = lax.axis_index("lon")
    has_up = lat < n_lat - 1
    has_dn = lat > 0
    right = lax.rem(lon + 1, n_lon)
    left = lax.rem(lon + n_lon - 1, n_lon)
    up_id = {"lon": lon, "lat": lat + 1}
    dn_id = {"lon": lon, "lat": lat - 1}
    right_id = {"lon": right, "lat": lat}
    left_id = {"lon": left, "lat": lat}

    water_copy = pltpu.make_async_copy(flat_hbm.at[1], water_buf, own_sem.at[0])
    water_copy.start()
    courant_copies = []
    for r in range(rows):
        courant_copies.append(
            pltpu.make_async_copy(courant_hbm.at[0, :, r, 0], c_east.at[r], own_sem.at[1 + r])
        )
        courant_copies.append(
            pltpu.make_async_copy(
                courant_hbm.at[1, :, r, 0], c_north.at[r + 1], own_sem.at[1 + rows + r]
            )
        )
    for copy in courant_copies:
        copy.start()
    base = 1 + 2 * rows

    def own_copy(f, r):
        return pltpu.make_async_copy(
            fields_hbm.at[f, :, r, 0], q_buf.at[f, HALO + r], own_sem.at[base + f * rows + r]
        )

    for f in range(nf):
        for r in range(rows):
            own_copy(f, r).start()

    barrier = pltpu.get_barrier_semaphore()
    pl.semaphore_signal(barrier, inc=1, device_id=right_id, device_id_type=MESH)
    pl.semaphore_signal(barrier, inc=1, device_id=left_id, device_id_type=MESH)

    @pl.when(has_up)
    def _():
        pl.semaphore_signal(barrier, inc=1, device_id=up_id, device_id_type=MESH)

    @pl.when(has_dn)
    def _():
        pl.semaphore_signal(barrier, inc=1, device_id=dn_id, device_id_type=MESH)

    pl.semaphore_wait(barrier, 2 + has_up.astype(jnp.int32) + has_dn.astype(jnp.int32))

    def z1_copy(f, side, r):
        if side == 0:
            source, target, device = rows - HALO + r, r, up_id
        else:
            source, target, device = r, HALO + rows + r, dn_id
        return pltpu.make_async_remote_copy(
            src_ref=fields_hbm.at[f, :, source, 0],
            dst_ref=q_buf.at[f, target],
            send_sem=z1_send.at[side, f, r],
            recv_sem=z1_recv.at[side, f, r],
            device_id=device,
            device_id_type=MESH,
        )

    def z2_copy(f, side):
        if side == 0:
            source, target, device = rows, 0, up_id
        else:
            source, target, device = HALO, HALO + rows, dn_id
        return pltpu.make_async_remote_copy(
            src_ref=s_buf.at[f, pl.ds(source, HALO)],
            dst_ref=s_buf.at[f, pl.ds(target, HALO)],
            send_sem=z2_send.at[side, f],
            recv_sem=z2_recv.at[side, f],
            device_id=device,
            device_id_type=MESH,
        )

    cn_copy = pltpu.make_async_remote_copy(
        src_ref=courant_hbm.at[1, :, rows - 1, 0],
        dst_ref=c_north.at[0],
        send_sem=cn_send,
        recv_sem=cn_recv,
        device_id=up_id,
        device_id_type=MESH,
    )

    def x_copy(n, side):
        return pltpu.make_async_remote_copy(
            src_ref=pack_send.at[side, n],
            dst_ref=pack_recv.at[side, n],
            send_sem=x_send.at[side, n],
            recv_sem=x_recv.at[side, n],
            device_id=right_id if side == 0 else left_id,
            device_id_type=MESH,
        )

    @pl.when(has_up)
    def _():
        cn_copy.start()

    @pl.loop(0, nf)
    def _(f):
        @pl.when(has_up)
        def _():
            for r in range(HALO):
                z1_copy(f, 0, r).start()

        @pl.when(has_dn)
        def _():
            for r in range(HALO):
                z1_copy(f, 1, r).start()

    zero = jnp.zeros((8, lanes), jnp.float32)

    def fill_zero(ref):
        for g in range(groups):
            ref[pl.ds(8 * g, 8), :] = zero

    @pl.when(jnp.logical_not(has_dn))
    def _():
        fill_zero(c_north.at[0])

        @pl.loop(0, nf)
        def _(f):
            for r in range(HALO):
                fill_zero(q_buf.at[f, r])
                fill_zero(s_buf.at[f, r])

    @pl.when(jnp.logical_not(has_up))
    def _():
        @pl.loop(0, nf)
        def _(f):
            for r in range(HALO):
                fill_zero(q_buf.at[f, HALO + rows + r])
                fill_zero(s_buf.at[f, HALO + rows + r])

    lane = lax.broadcasted_iota(jnp.int32, (8, lanes), 1)
    sub = lax.broadcasted_iota(jnp.int32, (8, lanes), 0)
    slot = lane >> 2
    own_half = (lane & 3) < 2
    low = sub < 4

    def pack(load):
        packed = zero
        for r in range(rows):
            for g in range(groups):
                k = r * groups + g
                packed = jnp.where(
                    slot == k, pltpu.roll(load(r, g), (4 * k + 2) % lanes, 1), packed
                )
        return packed

    def send_pair(n, even, odd):
        pack_send[0, n] = jnp.where(own_half, even, pltpu.roll(odd, 2, 1))
        pack_send[1, n] = jnp.where(own_half, pltpu.roll(even, lanes - 2, 1), odd)

    def recv_pair(n, odd):
        from_left = pack_recv[0, n]
        from_right = pack_recv[1, n]
        first = jnp.where(own_half, from_left, pltpu.roll(from_right, 2, 1))
        second = jnp.where(own_half, pltpu.roll(from_left, lanes - 2, 1), from_right)
        return jnp.where(odd, second, first)

    for copy in courant_copies:
        copy.wait()

    @pl.loop(0, nf)
    def _(f):
        for r in range(rows):
            own_copy(f, r).wait()
        pack_own[f] = pack(lambda r, g: q_buf[f, HALO + r, pl.ds(8 * g, 8), :])

    pairs_f = nf // 2
    c_slot = 2 * pairs_f
    c_pack = pack(lambda r, g: c_east[r, pl.ds(8 * g, 8), :])
    for n in range(pairs_f):
        send_pair(n, pack_own[2 * n], pack_own[2 * n + 1])
    send_pair(c_slot, c_pack, c_pack)
    for n in list(range(pairs_f)) + [c_slot]:
        x_copy(n, 0).start()
        x_copy(n, 1).start()

    cosz = jnp.concatenate([cosz_ref[...], cosz_ref[...]], axis=0)
    albedo = jnp.concatenate([albedo_ref[...], albedo_ref[...]], axis=0)
    neg_inv_mu = -1.0 / cosz
    ext = [
        jnp.where(low, ext_ref[2 * p], ext_ref[2 * p + 1]) * (4.0 / lev) for p in range(pairs)
    ]
    half_ssa = [jnp.where(low, ssa_ref[2 * p], ssa_ref[2 * p + 1]) * 0.5 for p in range(pairs)]
    weight = [jnp.where(low, weight_ref[2 * p], weight_ref[2 * p + 1]) for p in range(pairs)]

    ranks = lax.broadcasted_iota(jnp.int32, (lanes, lanes), 1)
    columns = lax.broadcasted_iota(jnp.int32, (lanes, lanes), 0)
    ones = jnp.ones((8, lanes), jnp.float32)
    sunlit = zero
    for r in range(rows):
        hit = (order_ref[r] == columns) & (ranks < count_ref[r, 0])
        row = lax.dot_general(
            ones,
            hit.astype(jnp.float32),
            (((1,), (1,)), ((), ())),
            preferred_element_type=jnp.float32,
        )
        sunlit = jnp.where((sub & 3) == r, row, sunlit)
    sunlit = sunlit * float(lev)

    water_copy.wait()

    def optics(k, beam):
        raw = water_buf[pl.ds(pl.multiple_of(8 * k, 8), 8), :]
        water = jnp.maximum(raw, 0.0) + jnp.log1p(jnp.exp(-jnp.abs(raw)))
        turned = pltpu.roll(water, 4, 0)
        for half in range(2):
            level = 2 * k + half
            here = jnp.where(low, water, turned) if half == 0 else jnp.where(low, turned, water)
            after = []
            for p in range(pairs):
                tau = ext[p] * here
                direct = jnp.exp(tau * neg_inv_mu)
                decay = jnp.exp(tau * -1.66)
                rad_a[level, p] = decay
                rad_b[level, p] = half_ssa[p] * (beam[p] * (1.0 - direct))
                rad_g[level, p] = beam[p]
                after.append(beam[p] * direct)
            beam = tuple(after)
        return beam

    beam = lax.fori_loop(0, lev // 2, optics, tuple(cosz for _ in range(pairs)))

    def up_level(i, carry):
        level = lev - 1 - i
        a_below, b_below = carry
        a_out, b_out = [], []
        for p in range(pairs):
            decay = rad_a[level, p]
            source = rad_b[level, p]
            reflect = half_ssa[p] * (1.0 - decay)
            transmit = decay + reflect
            inv = 1.0 / (1.0 - reflect * a_below[p])
            through = transmit * inv
            a_here = reflect + transmit * through * a_below[p]
            b_here = through * (a_below[p] * source + b_below[p]) + source
            rad_a[level, p] = through
            rad_b[level, p] = (reflect * b_below[p] + source) * inv
            rad_c[level, p] = weight[p] * (1.0 - a_here)
            rad_g[level, p] = weight[p] * (rad_g[level, p] - b_here)
            a_out.append(a_here)
            b_out.append(b_here)
        return tuple(a_out), tuple(b_out)

    floor_b = tuple(albedo * beam[p] for p in range(pairs))
    for p in range(pairs):
        rad_c[lev, p] = weight[p] * (1.0 - albedo)
        rad_g[lev, p] = weight[p] * (beam[p] - floor_b[p])
    lax.fori_loop(0, lev, up_level, (tuple(albedo for _ in range(pairs)), floor_b))

    def net_flux(level, down):
        total = rad_c[level, 0] * down[0] + rad_g[level, 0]
        for p in range(1, pairs):
            total = total + (rad_c[level, p] * down[p] + rad_g[level, p])
        return total + pltpu.roll(total, 4, 0)

    def down_pair(k, carry):
        down, net = carry
        heats = []
        for half in range(2):
            level = 2 * k + half
            down = tuple(rad_a[level, p] * down[p] + rad_b[level, p] for p in range(pairs))
            below = net_flux(level + 1, down)
            heats.append((net - below) * sunlit)
            net = below
        heat_buf[pl.ds(pl.multiple_of(8 * k, 8), 8), :] = jnp.where(low, heats[0], heats[1])
        return down, net

    start = tuple(zero for _ in range(pairs))
    lax.fori_loop(0, lev // 2, down_pair, (start, net_flux(0, start)))
    heat_copy = pltpu.make_async_copy(heat_buf, heat_hbm, out_sem.at[nf * rows])
    heat_copy.start()

    def x_wait(n):
        x_copy(n, 0).wait_recv()
        x_copy(n, 1).wait_recv()

    x_wait(c_slot)

    @pl.when(has_dn)
    def _():
        cn_copy.wait_recv()

    c_halo = recv_pair(c_slot, False)
    for r in range(rows):
        for g in range(groups):
            k = r * groups + g
            here = c_east[r, pl.ds(8 * g, 8), :]
            edge = pltpu.roll(c_halo, (lanes - 2 - 4 * k) % lanes, 1)
            west = pltpu.roll(jnp.where(lane == lanes - 1, edge, here), 1, 1)
            c_west[r, pl.ds(8 * g, 8), :] = west * (1.0 / 12.0)
            c_east[r, pl.ds(8 * g, 8), :] = here * (1.0 / 12.0)
    for r in range(rows + 1):
        for g in range(groups):
            c_north[r, pl.ds(8 * g, 8), :] = c_north[r, pl.ds(8 * g, 8), :] * (1.0 / 12.0)

    first_lane = lane == 0
    first_two = lane < 2
    last_lane = lane == lanes - 1
    last_two = lane >= lanes - 2

    def tendency(buf, f, halo, emit):
        for g in range(groups):
            at = pl.ds(8 * g, 8)
            q = [buf[f, j, at, :] for j in range(rows + 2 * HALO)]
            north = [
                c_north[j, at, :] * (7.0 * (q[j + 1] + q[j + 2]) - (q[j] + q[j + 3]))
                for j in range(rows + 1)
            ]
            for r in range(rows):
                k = r * groups + g
                here = q[r + HALO]
                edge = pltpu.roll(halo, (lanes - 2 - 4 * k) % lanes, 1)
                r1 = pltpu.roll(jnp.where(first_lane, edge, here), lanes - 1, 1)
                r2 = pltpu.roll(jnp.where(first_two, edge, here), lanes - 2, 1)
                l1 = pltpu.roll(jnp.where(last_lane, edge, here), 1, 1)
                l2 = pltpu.roll(jnp.where(last_two, edge, here), 2, 1)
                east = c_east[r, at, :] * (7.0 * (here + r1) - (l1 + r2))
                west = c_west[r, at, :] * (7.0 * (l1 + here) - (l2 + r1))
                emit(r, g, here, -((east - west) + (north[r + 1] - north[r])))

    def z1_wait(f):
        @pl.when(has_dn)
        def _():
            for r in range(HALO):
                z1_copy(f, 0, r).wait_recv()

        @pl.when(has_up)
        def _():
            for r in range(HALO):
                z1_copy(f, 1, r).wait_recv()

    for n in range(pairs_f):
        x_wait(n)

    @pl.loop(0, pairs_f)
    def _(n):
        packed = []
        for odd in range(2):
            f = 2 * n + odd
            z1_wait(f)

            def emit(r, g, here, change):
                s_buf[f, HALO + r, pl.ds(8 * g, 8), :] = here + change

            tendency(q_buf, f, recv_pair(n, odd == 1), emit)
            packed.append(pack(lambda r, g: s_buf[f, HALO + r, pl.ds(8 * g, 8), :]))

            @pl.when(has_up)
            def _():
                z2_copy(f, 0).start()

            @pl.when(has_dn)
            def _():
                z2_copy(f, 1).start()

        m = pairs_f + n
        send_pair(m, packed[0], packed[1])
        x_copy(m, 0).start()
        x_copy(m, 1).start()

    def out_copy(f, r):
        return pltpu.make_async_copy(
            o_buf.at[f, r], out_hbm.at[f, :, r, 0], out_sem.at[f * rows + r]
        )

    def final(f, halo, extra):
        def emit(r, g, here, change):
            value = 0.5 * ((q_buf[f, HALO + r, pl.ds(8 * g, 8), :] + here) + change)
            if extra:
                value = value + 0.5 * heat_buf[pl.ds(8 * rows * g + r, 8, stride=rows), :]
            o_buf[f, r, pl.ds(8 * g, 8), :] = value

        @pl.when(has_dn)
        def _():
            z2_copy(f, 0).wait_recv()

        @pl.when(has_up)
        def _():
            z2_copy(f, 1).wait_recv()

        tendency(s_buf, f, halo, emit)
        for r in range(rows):
            out_copy(f, r).start()

    x_wait(pairs_f)
    final(0, recv_pair(pairs_f, False), True)

    @pl.loop(1, nf)
    def _(f):
        n = pairs_f + f // 2

        @pl.when(f % 2 == 0)
        def _():
            x_wait(n)

        final(f, recv_pair(n, f % 2 == 1), False)

    heat_copy.wait()

    @pl.loop(0, nf)
    def _(f):
        for r in range(rows):
            out_copy(f, r).wait()

        @pl.when(has_up)
        def _():
            for r in range(HALO):
                z1_copy(f, 0, r).wait_send()
            z2_copy(f, 0).wait_send()

        @pl.when(has_dn)
        def _():
            for r in range(HALO):
                z1_copy(f, 1, r).wait_send()
            z2_copy(f, 1).wait_send()

    @pl.when(has_up)
    def _():
        cn_copy.wait_send()

    for n in range(2 * pairs_f + 1):
        x_copy(n, 0).wait_send()
        x_copy(n, 1).wait_send()


def per_device(n_lat, n_lon, fields, courant, cosz, albedo, ext, ssa, weight, order, count):
    nf, lev, rows, lanes = fields.shape
    bands = ext.shape[0]
    dims = (nf, lev, rows, lanes, bands, n_lat, n_lon)
    tall = rows + 2 * HALO
    f32 = jnp.float32
    any_spec = pl.BlockSpec(memory_space=pl.ANY)
    vmem_spec = pl.BlockSpec(memory_space=pltpu.VMEM)
    smem_spec = pl.BlockSpec(memory_space=pltpu.SMEM)
    rad = pltpu.VMEM((lev + 1, bands // 2, 8, lanes), f32)
    packs = nf + 1
    out, heat = pl.pallas_call(
        functools.partial(step_kernel, dims),
        out_shape=(
            jax.ShapeDtypeStruct((nf, lev, rows, 1, lanes), f32),
            jax.ShapeDtypeStruct((lev * rows, lanes), f32),
        ),
        in_specs=[any_spec] * 3
        + [vmem_spec] * 2
        + [smem_spec] * 3
        + [vmem_spec, smem_spec],
        out_specs=(any_spec, any_spec),
        scratch_shapes=[
            pltpu.VMEM((nf, tall, lev, lanes), f32),
            pltpu.VMEM((nf, tall, lev, lanes), f32),
            pltpu.VMEM((nf, rows, lev, lanes), f32),
            pltpu.VMEM((rows, lev, lanes), f32),
            pltpu.VMEM((rows, lev, lanes), f32),
            pltpu.VMEM((rows + 1, lev, lanes), f32),
            pltpu.VMEM((lev * rows, lanes), f32),
            pltpu.VMEM((lev * rows, lanes), f32),
            rad,
            rad,
            rad,
            rad,
            pltpu.VMEM((nf, 8, lanes), f32),
            pltpu.VMEM((2, packs, 8, lanes), f32),
            pltpu.VMEM((2, packs, 8, lanes), f32),
            pltpu.SemaphoreType.DMA((1 + 2 * rows + nf * rows,)),
            pltpu.SemaphoreType.DMA((nf * rows + 1,)),
            pltpu.SemaphoreType.DMA((2, nf, HALO)),
            pltpu.SemaphoreType.DMA((2, nf, HALO)),
            pltpu.SemaphoreType.DMA((2, nf)),
            pltpu.SemaphoreType.DMA((2, nf)),
            pltpu.SemaphoreType.DMA,
            pltpu.SemaphoreType.DMA,
            pltpu.SemaphoreType.DMA((2, packs)),
            pltpu.SemaphoreType.DMA((2, packs)),
        ],
        compiler_params=pltpu.CompilerParams(
            collective_id=0, has_side_effects=True, vmem_limit_bytes=48 * 1024 * 1024
        ),
        name="advect_radiate",
    )(
        fields.reshape(nf, lev, rows, 1, lanes),
        fields.reshape(nf, lev * rows, lanes),
        courant.reshape(2, lev, rows, 1, lanes),
        cosz,
        albedo,
        ext,
        ssa,
        weight,
        order,
        count,
    )
    return out.reshape(nf, lev, rows, lanes), heat.reshape(lev, rows, lanes)


def solution(mesh):
    n_lat, n_lon = mesh.shape["lat"], mesh.shape["lon"]
    in_specs = (
        P(None, None, "lat", "lon"),
        P(None, None, "lat", "lon"),
        P("lat", "lon"),
        P("lat", "lon"),
        P(),
        P(),
        P(),
        P("lat", "lon", None),
        P("lat", "lon"),
    )
    out_specs = (P(None, None, "lat", "lon"), P(None, "lat", "lon"))
    return jax.shard_map(
        functools.partial(per_device, n_lat, n_lon),
        mesh=mesh,
        in_specs=in_specs,
        out_specs=out_specs,
        check_vma=False,
    )
```

profile of v0, /device:TPU:32, one launch (start us, length us, event | category | flops | bytes accessed | tf_op | source)
XLA Modules:
  0.0 49.1 jit_solution(4498065549668431994)
XLA Ops:
  0.6 0.0 copy-start.8
  0.6 0.0 copy-start.5
  0.7 0.0 copy-start.6
  0.7 0.0 copy-start.7
  0.7 0.0 copy-start.4
  0.7 0.0 copy-start.2
  0.7 0.0 copy-start.3
  0.7 0.6 %copy-done.8 = s32[4,1]{0,1:T(1,128)S(1)} copy-done((s32[4,1]{0,1:T(1,128)S(1)}, s32[4,1]{0,1:T(1,128)}, u32[]{:S(2)}) %copy-start.8) | copy-done | bytes 40
  1.3 0.1 copy.11.count_ref
  1.4 0.0 copy-done.5
  1.4 0.0 copy-done.6
  1.4 0.0 copy-done.7
  1.4 0.0 copy-done.4
  1.4 0.0 copy-done.2
  1.4 0.0 copy-done.3
  1.4 0.0 copy-start
  1.4 1.2 %copy-done = f32[8,64,4,128]{3,2,1,0:T(4,128)S(1)} copy-done((f32[8,64,4,128]{3,2,1,0:T(4,128)S(1)}, f32[8,64,4,128]{3,2,1,0:T(4,128)}, u32[]{:S(2)}) %copy-start) | copy-done | bytes 1048600
  2.6 0.0 copy-start.1
  2.6 0.9 %copy-done.1 = f32[2,64,4,128]{3,2,1,0:T(4,128)S(1)} copy-done((f32[2,64,4,128]{3,2,1,0:T(4,128)S(1)}, f32[2,64,4,128]{3,2,1,0:T(4,128)}, u32[]{:S(2)}) %copy-start.1) | copy-done | bytes 262168
  3.6 43.8 %advect_radiate.1 = (f32[8,64,4,1,128]{4,3,2,1,0:T(1,128)S(1)}, f32[256,128]{1,0:T(8,128)S(1)}) custom-call(f32[8,64,4,1,128]{4,3,2,1,0:T(1,128)S(1)} %bitcast.5, f32[8,256,128]{2,1,0:T(8,128)S(1)} %bitcast.6, f32[2,64,4,1,128]{4,3,2,1,0:T(1,128)S(1)} %bitcast.8, f32[4,128]{1,0:T(4,128)S(1)} %copy-done.2, f32[4,128]{1,0:T(4,128)S(1)} %copy-done.3, ...), custom_call_target="tpu_custom_call" | custom-call | tf_op jit(solution)/shard_map/advect_radiate/pallas_call | solution.py:501
  47.4 1.0 %copy.14 = f32[8,64,4,128]{3,2,1,0:T(4,128)} copy(f32[8,64,4,128]{3,2,1,0:T(4,128)S(1)} %bitcast.7) | data formatting | bytes 2097152
  48.4 0.7 %copy.15 = f32[64,4,128]{2,1,0:T(4,128)} copy(f32[64,4,128]{2,1,0:T(4,128)S(1)} %bitcast.9) | data formatting | bytes 262144
Async XLA Ops:
  0.6 0.7 %copy-start.8 = (s32[4,1]{0,1:T(1,128)S(1)}, s32[4,1]{0,1:T(1,128)}, u32[]{:S(2)}) copy-start(s32[4,1]{0,1:T(1,128)} %param.17) | copy-start | bytes 52
  0.6 0.7 %copy-start.5 = (f32[14]{0:T(128)S(1)}, f32[14]{0:T(128)}, u32[]{:S(2)}) copy-start(f32[14]{0:T(128)} %ext_ref.1) | copy-start | bytes 172
  0.7 0.7 %copy-start.6 = (f32[14]{0:T(128)S(1)}, f32[14]{0:T(128)}, u32[]{:S(2)}) copy-start(f32[14]{0:T(128)} %ssa_ref.1) | copy-start | bytes 172
  0.7 0.7 %copy-start.7 = (f32[14]{0:T(128)S(1)}, f32[14]{0:T(128)}, u32[]{:S(2)}) copy-start(f32[14]{0:T(128)} %weight_ref.1) | copy-start | bytes 172
  0.7 0.7 %copy-start.4 = (s32[4,1,128]{2,1,0:T(1,128)S(1)}, s32[4,1,128]{2,1,0:T(1,128)}, u32[]{:S(2)}) copy-start(s32[4,1,128]{2,1,0:T(1,128)} %order_ref.1) | copy-start | bytes 6148
  0.7 0.7 %copy-start.2 = (f32[4,128]{1,0:T(4,128)S(1)}, f32[4,128]{1,0:T(4,128)}, u32[]{:S(2)}) copy-start(f32[4,128]{1,0:T(4,128)} %cosz_ref.1) | copy-start | bytes 6148
  0.7 0.7 %copy-start.3 = (f32[4,128]{1,0:T(4,128)S(1)}, f32[4,128]{1,0:T(4,128)}, u32[]{:S(2)}) copy-start(f32[4,128]{1,0:T(4,128)} %albedo_ref.1) | copy-start | bytes 6148
  1.4 1.2 %copy-start = (f32[8,64,4,128]{3,2,1,0:T(4,128)S(1)}, f32[8,64,4,128]{3,2,1,0:T(4,128)}, u32[]{:S(2)}) copy-start(f32[8,64,4,128]{3,2,1,0:T(4,128)} %param.9) | copy-start | bytes 3145732
  2.6 0.9 %copy-start.1 = (f32[2,64,4,128]{3,2,1,0:T(4,128)S(1)}, f32[2,64,4,128]{3,2,1,0:T(4,128)}, u32[]{:S(2)}) copy-start(f32[2,64,4,128]{3,2,1,0:T(4,128)} %param.10) | copy-start | bytes 786436
where the time goes:
time: 49.2 us; the launch traced here: 49.1 us
  Pallas kernels  43.8 us (89%)
  local copies, waits for them, and re-layouts  4.5 us (9%)
  between operations  0.73 us (1%)
    pallas_call x1, Pallas kernels, per_device(): pl.pallas_call(functools.partial(step_kernel, dims), out_shape=(jax.Shape...  43.8 us
    unnamed x21, local copies, waits for them, and re-layouts  4.5 us

commit v1 on v0

--- a/solution.py
+++ b/solution.py
@@ -16,6 +16,23 @@
     fields_hbm,
     flat_hbm,
     courant_hbm,
+    c_flat_hbm,
+    cosz_hbm,
+    albedo_hbm,
+    ext_hbm,
+    ssa_hbm,
+    weight_hbm,
+    order_hbm,
+    count_hbm,
+    out_ref,
+    heat_ref,
+    q_buf,
+    q_halo,
+    s_buf,
+    c_buf,
+    c_east,
+    c_west,
+    c_north,
     cosz_ref,
     albedo_ref,
     ext_ref,
@@ -23,16 +40,6 @@
     weight_ref,
     order_ref,
     count_ref,
-    out_hbm,
-    heat_hbm,
-    q_buf,
-    s_buf,
-    o_buf,
-    c_east,
-    c_west,
-    c_north,
-    water_buf,
-    heat_buf,
     rad_a,
     rad_b,
     rad_c,
@@ -41,7 +48,8 @@
     pack_send,
     pack_recv,
     own_sem,
-    out_sem,
+    small_sem,
+    go_sem,
     z1_send,
     z1_recv,
     z2_send,
@@ -65,53 +73,106 @@
     right_id = {"lon": right, "lat": lat}
     left_id = {"lon": left, "lat": lat}
 
-    water_copy = pltpu.make_async_copy(flat_hbm.at[1], water_buf, own_sem.at[0])
-    water_copy.start()
-    courant_copies = []
-    for r in range(rows):
-        courant_copies.append(
-            pltpu.make_async_copy(courant_hbm.at[0, :, r, 0], c_east.at[r], own_sem.at[1 + r])
+    half = n_lon // 2
+    place = lax.rem(lon, half)
+    far_right = place == half - 1
+    far_left = place == 0
+    is_far = far_right | far_left
+    is_near = jnp.logical_not(is_far)
+    far = jnp.where(far_right, right, left)
+    partner = jnp.where(far_right, left, right)
+    by_right_end = place == half - 2
+    by_left_end = place == 1
+    is_partner = by_right_end | by_left_end
+    end = jnp.where(by_right_end, right, left)
+    late_half = lon >= half
+    early_half = jnp.logical_not(late_half)
+
+    def field_copy(f):
+        return pltpu.make_async_copy(flat_hbm.at[f], q_buf.at[f], own_sem.at[f])
+
+    c_copy = pltpu.make_async_copy(c_flat_hbm, c_buf, own_sem.at[nf])
+    small = [
+        pltpu.make_async_copy(source, target, small_sem.at[i])
+        for i, (source, target) in enumerate(
+            [
+                (cosz_hbm, cosz_ref),
+                (albedo_hbm, albedo_ref),
+                (ext_hbm, ext_ref),
+                (ssa_hbm, ssa_ref),
+                (weight_hbm, weight_ref),
+                (order_hbm, order_ref),
+                (count_hbm, count_ref),
+            ]
         )
-        courant_copies.append(
-            pltpu.make_async_copy(
-                courant_hbm.at[1, :, r, 0], c_north.at[r + 1], own_sem.at[1 + rows + r]
+    ]
+
+    barrier = pltpu.get_barrier_semaphore()
+
+    def greet(device):
+        pl.semaphore_signal(barrier, inc=1, device_id=device, device_id_type=MESH)
+
+    @pl.when(is_far)
+    def _():
+        greet({"lon": partner, "lat": lat})
+        greet({"lon": far, "lat": lat})
+
+        @pl.when(has_up)
+        def _():
+            greet({"lon": partner, "lat": lat + 1})
+
+        @pl.when(has_dn)
+        def _():
+            greet({"lon": partner, "lat": lat - 1})
+
+    @pl.when(is_near)
+    def _():
+        @pl.when(has_up)
+        def _():
+            greet(up_id)
+
+        @pl.when(has_dn)
+        def _():
+            greet(dn_id)
+
+        @pl.when(jnp.logical_not(by_right_end))
+        def _():
+            greet(right_id)
+
+        @pl.when(jnp.logical_not(by_left_end))
+        def _():
+            greet(left_id)
+
+    for f in range(nf):
+        field_copy(f).start()
+    c_copy.start()
+    for copy in small:
+        copy.start()
+
+    n_beside = has_up.astype(jnp.int32) + has_dn.astype(jnp.int32)
+
+    @pl.when(is_near)
+    def _():
+        pl.semaphore_wait(barrier, 2 + n_beside + jnp.where(is_partner, n_beside, 0))
+
+        @pl.when(is_partner)
+        def _():
+            pl.semaphore_signal(
+                go_sem, inc=1, device_id={"lon": end, "lat": lat}, device_id_type=MESH
             )
-        )
-    for copy in courant_copies:
-        copy.start()
-    base = 1 + 2 * rows
-
-    def own_copy(f, r):
-        return pltpu.make_async_copy(
-            fields_hbm.at[f, :, r, 0], q_buf.at[f, HALO + r], own_sem.at[base + f * rows + r]
-        )
-
-    for f in range(nf):
-        for r in range(rows):
-            own_copy(f, r).start()
-
-    barrier = pltpu.get_barrier_semaphore()
-    pl.semaphore_signal(barrier, inc=1, device_id=right_id, device_id_type=MESH)
-    pl.semaphore_signal(barrier, inc=1, device_id=left_id, device_id_type=MESH)
-
-    @pl.when(has_up)
-    def _():
-        pl.semaphore_signal(barrier, inc=1, device_id=up_id, device_id_type=MESH)
-
-    @pl.when(has_dn)
-    def _():
-        pl.semaphore_signal(barrier, inc=1, device_id=dn_id, device_id_type=MESH)
-
-    pl.semaphore_wait(barrier, 2 + has_up.astype(jnp.int32) + has_dn.astype(jnp.int32))
+
+    @pl.when(is_far)
+    def _():
+        pl.semaphore_wait(go_sem, 1)
 
     def z1_copy(f, side, r):
         if side == 0:
             source, target, device = rows - HALO + r, r, up_id
         else:
-            source, target, device = r, HALO + rows + r, dn_id
+            source, target, device = r, HALO + r, dn_id
         return pltpu.make_async_remote_copy(
             src_ref=fields_hbm.at[f, :, source, 0],
-            dst_ref=q_buf.at[f, target],
+            dst_ref=q_halo.at[f, target],
             send_sem=z1_send.at[side, f, r],
             recv_sem=z1_recv.at[side, f, r],
             device_id=device,
@@ -180,7 +241,7 @@
         @pl.loop(0, nf)
         def _(f):
             for r in range(HALO):
-                fill_zero(q_buf.at[f, r])
+                fill_zero(q_halo.at[f, r])
                 fill_zero(s_buf.at[f, r])
 
     @pl.when(jnp.logical_not(has_up))
@@ -188,7 +249,7 @@
         @pl.loop(0, nf)
         def _(f):
             for r in range(HALO):
-                fill_zero(q_buf.at[f, HALO + rows + r])
+                fill_zero(q_halo.at[f, HALO + r])
                 fill_zero(s_buf.at[f, HALO + rows + r])
 
     lane = lax.broadcasted_iota(jnp.int32, (8, lanes), 1)
@@ -218,25 +279,46 @@
         second = jnp.where(own_half, pltpu.roll(from_left, lanes - 2, 1), from_right)
         return jnp.where(odd, second, first)
 
-    for copy in courant_copies:
-        copy.wait()
+    def own_row(f, r, g):
+        return q_buf[f, pl.ds(8 * rows * g + r, 8, stride=rows), :]
 
     @pl.loop(0, nf)
     def _(f):
-        for r in range(rows):
-            own_copy(f, r).wait()
-        pack_own[f] = pack(lambda r, g: q_buf[f, HALO + r, pl.ds(8 * g, 8), :])
-
+        field_copy(f).wait()
+        pack_own[f] = pack(lambda r, g: own_row(f, r, g))
+
+    c_copy.wait()
     pairs_f = nf // 2
     c_slot = 2 * pairs_f
-    c_pack = pack(lambda r, g: c_east[r, pl.ds(8 * g, 8), :])
+    c_pack = pack(lambda r, g: c_buf[0, pl.ds(8 * rows * g + r, 8, stride=rows), :])
     for n in range(pairs_f):
         send_pair(n, pack_own[2 * n], pack_own[2 * n + 1])
     send_pair(c_slot, c_pack, c_pack)
-    for n in list(range(pairs_f)) + [c_slot]:
-        x_copy(n, 0).start()
-        x_copy(n, 1).start()
-
+    first_slots = list(range(pairs_f)) + [c_slot]
+
+    def send_first(where, sides):
+        for side in sides:
+            @pl.when(where & jnp.logical_not(far_right if side == 0 else far_left))
+            def _():
+                for n in first_slots:
+                    x_copy(n, side).start()
+
+    def send_far(where):
+        @pl.when(where & is_far)
+        def _():
+            pl.semaphore_wait(barrier, 1)
+
+        for side in range(2):
+            @pl.when(where & (far_right if side == 0 else far_left))
+            def _():
+                for n in first_slots:
+                    x_copy(n, side).start()
+
+    send_first(lon >= 0, (0, 1))
+    send_far(late_half)
+
+    for copy in small:
+        copy.wait()
     cosz = jnp.concatenate([cosz_ref[...], cosz_ref[...]], axis=0)
     albedo = jnp.concatenate([albedo_ref[...], albedo_ref[...]], axis=0)
     neg_inv_mu = -1.0 / cosz
@@ -251,7 +333,7 @@
     ones = jnp.ones((8, lanes), jnp.float32)
     sunlit = zero
     for r in range(rows):
-        hit = (order_ref[r] == columns) & (ranks < count_ref[r, 0])
+        hit = (order_ref[r] == columns) & (ranks < count_ref[r])
         row = lax.dot_general(
             ones,
             hit.astype(jnp.float32),
@@ -261,10 +343,8 @@
         sunlit = jnp.where((sub & 3) == r, row, sunlit)
     sunlit = sunlit * float(lev)
 
-    water_copy.wait()
-
     def optics(k, beam):
-        raw = water_buf[pl.ds(pl.multiple_of(8 * k, 8), 8), :]
+        raw = q_buf[1, pl.ds(pl.multiple_of(8 * k, 8), 8), :]
         water = jnp.maximum(raw, 0.0) + jnp.log1p(jnp.exp(-jnp.abs(raw)))
         turned = pltpu.roll(water, 4, 0)
         for half in range(2):
@@ -326,13 +406,12 @@
             below = net_flux(level + 1, down)
             heats.append((net - below) * sunlit)
             net = below
-        heat_buf[pl.ds(pl.multiple_of(8 * k, 8), 8), :] = jnp.where(low, heats[0], heats[1])
+        heat_ref[pl.ds(pl.multiple_of(8 * k, 8), 8), :] = jnp.where(low, heats[0], heats[1])
         return down, net
 
     start = tuple(zero for _ in range(pairs))
     lax.fori_loop(0, lev // 2, down_pair, (start, net_flux(0, start)))
-    heat_copy = pltpu.make_async_copy(heat_buf, heat_hbm, out_sem.at[nf * rows])
-    heat_copy.start()
+    send_far(early_half)
 
     def x_wait(n):
         x_copy(n, 0).wait_recv()
@@ -348,24 +427,25 @@
     for r in range(rows):
         for g in range(groups):
             k = r * groups + g
-            here = c_east[r, pl.ds(8 * g, 8), :]
+            here = c_buf[0, pl.ds(8 * rows * g + r, 8, stride=rows), :]
             edge = pltpu.roll(c_halo, (lanes - 2 - 4 * k) % lanes, 1)
             west = pltpu.roll(jnp.where(lane == lanes - 1, edge, here), 1, 1)
             c_west[r, pl.ds(8 * g, 8), :] = west * (1.0 / 12.0)
             c_east[r, pl.ds(8 * g, 8), :] = here * (1.0 / 12.0)
-    for r in range(rows + 1):
-        for g in range(groups):
-            c_north[r, pl.ds(8 * g, 8), :] = c_north[r, pl.ds(8 * g, 8), :] * (1.0 / 12.0)
+            north = c_buf[1, pl.ds(8 * rows * g + r, 8, stride=rows), :]
+            c_north[r + 1, pl.ds(8 * g, 8), :] = north * (1.0 / 12.0)
+    for g in range(groups):
+        c_north[0, pl.ds(8 * g, 8), :] = c_north[0, pl.ds(8 * g, 8), :] * (1.0 / 12.0)
 
     first_lane = lane == 0
     first_two = lane < 2
     last_lane = lane == lanes - 1
     last_two = lane >= lanes - 2
 
-    def tendency(buf, f, halo, emit):
+    def tendency(load, halo, emit):
         for g in range(groups):
             at = pl.ds(8 * g, 8)
-            q = [buf[f, j, at, :] for j in range(rows + 2 * HALO)]
+            q = [load(j, g, at) for j in range(rows + 2 * HALO)]
             north = [
                 c_north[j, at, :] * (7.0 * (q[j + 1] + q[j + 2]) - (q[j] + q[j + 3]))
                 for j in range(rows + 1)
@@ -406,7 +486,14 @@
             def emit(r, g, here, change):
                 s_buf[f, HALO + r, pl.ds(8 * g, 8), :] = here + change
 
-            tendency(q_buf, f, recv_pair(n, odd == 1), emit)
+            def load(j, g, at):
+                if j < HALO:
+                    return q_halo[f, j, at, :]
+                if j < HALO + rows:
+                    return own_row(f, j - HALO, g)
+                return q_halo[f, j - rows, at, :]
+
+            tendency(load, recv_pair(n, odd == 1), emit)
             packed.append(pack(lambda r, g: s_buf[f, HALO + r, pl.ds(8 * g, 8), :]))
 
             @pl.when(has_up)
@@ -422,17 +509,12 @@
         x_copy(m, 0).start()
         x_copy(m, 1).start()
 
-    def out_copy(f, r):
-        return pltpu.make_async_copy(
-            o_buf.at[f, r], out_hbm.at[f, :, r, 0], out_sem.at[f * rows + r]
-        )
-
     def final(f, halo, extra):
         def emit(r, g, here, change):
-            value = 0.5 * ((q_buf[f, HALO + r, pl.ds(8 * g, 8), :] + here) + change)
+            value = 0.5 * ((own_row(f, r, g) + here) + change)
             if extra:
-                value = value + 0.5 * heat_buf[pl.ds(8 * rows * g + r, 8, stride=rows), :]
-            o_buf[f, r, pl.ds(8 * g, 8), :] = value
+                value = value + 0.5 * heat_ref[pl.ds(8 * rows * g + r, 8, stride=rows), :]
+            out_ref[f, pl.ds(8 * rows * g + r, 8, stride=rows), :] = value
 
         @pl.when(has_dn)
         def _():
@@ -442,9 +524,7 @@
         def _():
             z2_copy(f, 1).wait_recv()
 
-        tendency(s_buf, f, halo, emit)
-        for r in range(rows):
-            out_copy(f, r).start()
+        tendency(lambda j, g, at: s_buf[f, j, at, :], halo, emit)
 
     x_wait(pairs_f)
     final(0, recv_pair(pairs_f, False), True)
@@ -459,13 +539,8 @@
 
         final(f, recv_pair(n, f % 2 == 1), False)
 
-    heat_copy.wait()
-
     @pl.loop(0, nf)
     def _(f):
-        for r in range(rows):
-            out_copy(f, r).wait()
-
         @pl.when(has_up)
         def _():
             for r in range(HALO):
@@ -485,6 +560,17 @@
     for n in range(2 * pairs_f + 1):
         x_copy(n, 0).wait_send()
         x_copy(n, 1).wait_send()
+
+
+def store_kernel(parts, new_ref, heat_ref, new_hbm, out_heat_hbm, sem):
+    copies = [
+        pltpu.make_async_copy(new_ref.at[f], new_hbm.at[f], sem.at[f]) for f in range(parts)
+    ]
+    copies.append(pltpu.make_async_copy(heat_ref, out_heat_hbm, sem.at[parts]))
+    for copy in copies:
+        copy.start()
+    for copy in copies:
+        copy.wait()
 
 
 def per_device(n_lat, n_lon, fields, courant, cosz, albedo, ext, ssa, weight, order, count):
@@ -493,31 +579,37 @@
     dims = (nf, lev, rows, lanes, bands, n_lat, n_lon)
     tall = rows + 2 * HALO
     f32 = jnp.float32
-    any_spec = pl.BlockSpec(memory_space=pl.ANY)
+    hbm_spec = pl.BlockSpec(memory_space=pltpu.HBM)
     vmem_spec = pl.BlockSpec(memory_space=pltpu.VMEM)
-    smem_spec = pl.BlockSpec(memory_space=pltpu.SMEM)
     rad = pltpu.VMEM((lev + 1, bands // 2, 8, lanes), f32)
     packs = nf + 1
+    results = (
+        jax.ShapeDtypeStruct((nf, lev * rows, lanes), f32),
+        jax.ShapeDtypeStruct((lev * rows, lanes), f32),
+    )
     out, heat = pl.pallas_call(
         functools.partial(step_kernel, dims),
         out_shape=(
-            jax.ShapeDtypeStruct((nf, lev, rows, 1, lanes), f32),
-            jax.ShapeDtypeStruct((lev * rows, lanes), f32),
+            pltpu.VMEM((nf, lev * rows, lanes), f32),
+            pltpu.VMEM((lev * rows, lanes), f32),
         ),
-        in_specs=[any_spec] * 3
-        + [vmem_spec] * 2
-        + [smem_spec] * 3
-        + [vmem_spec, smem_spec],
-        out_specs=(any_spec, any_spec),
+        in_specs=[hbm_spec] * 11,
+        out_specs=(vmem_spec, vmem_spec),
         scratch_shapes=[
+            pltpu.VMEM((nf, lev * rows, lanes), f32),
+            pltpu.VMEM((nf, 2 * HALO, lev, lanes), f32),
             pltpu.VMEM((nf, tall, lev, lanes), f32),
-            pltpu.VMEM((nf, tall, lev, lanes), f32),
-            pltpu.VMEM((nf, rows, lev, lanes), f32),
+            pltpu.VMEM((2, lev * rows, lanes), f32),
             pltpu.VMEM((rows, lev, lanes), f32),
             pltpu.VMEM((rows, lev, lanes), f32),
             pltpu.VMEM((rows + 1, lev, lanes), f32),
-            pltpu.VMEM((lev * rows, lanes), f32),
-            pltpu.VMEM((lev * rows, lanes), f32),
+            pltpu.VMEM((rows, lanes), f32),
+            pltpu.VMEM((rows, lanes), f32),
+            pltpu.SMEM((bands,), f32),
+            pltpu.SMEM((bands,), f32),
+            pltpu.SMEM((bands,), f32),
+            pltpu.VMEM((rows, 1, lanes), jnp.int32),
+            pltpu.SMEM((rows,), jnp.int32),
             rad,
             rad,
             rad,
@@ -525,8 +617,9 @@
             pltpu.VMEM((nf, 8, lanes), f32),
             pltpu.VMEM((2, packs, 8, lanes), f32),
             pltpu.VMEM((2, packs, 8, lanes), f32),
-            pltpu.SemaphoreType.DMA((1 + 2 * rows + nf * rows,)),
-            pltpu.SemaphoreType.DMA((nf * rows + 1,)),
+            pltpu.SemaphoreType.DMA((nf + 1,)),
+            pltpu.SemaphoreType.DMA((7,)),
+            pltpu.SemaphoreType.REGULAR,
             pltpu.SemaphoreType.DMA((2, nf, HALO)),
             pltpu.SemaphoreType.DMA((2, nf, HALO)),
             pltpu.SemaphoreType.DMA((2, nf)),
@@ -541,17 +634,32 @@
         ),
         name="advect_radiate",
     )(
-        fields.reshape(nf, lev, rows, 1, lanes),
-        fields.reshape(nf, lev * rows, lanes),
-        courant.reshape(2, lev, rows, 1, lanes),
-        cosz,
-        albedo,
-        ext,
-        ssa,
-        weight,
-        order,
-        count,
+        *(
+            pltpu.with_memory_space_constraint(x, pltpu.HBM)
+            for x in (
+                fields.reshape(nf, lev, rows, 1, lanes),
+                fields.reshape(nf, lev * rows, lanes),
+                courant.reshape(2, lev, rows, 1, lanes),
+                courant.reshape(2, lev * rows, lanes),
+                cosz,
+                albedo,
+                ext,
+                ssa,
+                weight,
+                order,
+                count.reshape(rows),
+            )
+        )
     )
+    out, heat = pl.pallas_call(
+        functools.partial(store_kernel, nf),
+        out_shape=results,
+        in_specs=[pl.BlockSpec(memory_space=pl.ANY)] * 2,
+        out_specs=(hbm_spec, hbm_spec),
+        scratch_shapes=[pltpu.SemaphoreType.DMA((nf + 1,))],
+        compiler_params=pltpu.CompilerParams(vmem_limit_bytes=32 * 1024 * 1024),
+        name="store_results",
+    )(out, heat)
     return out.reshape(nf, lev, rows, lanes), heat.reshape(lev, rows, lanes)
 
 

time: 49.2 us -> 41.5 us (0.84)
  local copies, waits for them, and re-layouts: 4.5 us -> 0 us
  Pallas kernels: 43.8 us -> 40.7 us
    unnamed x21 -> x0, local copies, waits for them, and re-layouts: 4.5 us -> none
    pallas_call x1 -> x2, Pallas kernels: 43.8 us -> 40.7 us  [the longest x1 39.6 us: per_device(): pl.pallas_call(functools.partial(step_kernel, dims), out_shape=(pltpu.VME...]
where the time goes in v1:
time: 41.5 us; the launch traced here: 41.4 us
  Pallas kernels  40.7 us (98%)
  between operations  0.64 us (2%)
    pallas_call x1, Pallas kernels, per_device(): pl.pallas_call(functools.partial(step_kernel, dims), out_shape=(pltpu.VME...  39.6 us
    pallas_call x1, Pallas kernels, per_device(): pl.pallas_call(functools.partial(store_kernel, nf), out_shape=results, in...  1.08 us

profile of v1, /device:TPU:32, one launch (start us, length us, event | category | flops | bytes accessed | tf_op | source)
XLA Modules:
  0.0 41.4 jit_solution(14921646684952625606)
XLA Ops:
  0.6 39.6 %advect_radiate.1 = (f32[8,256,128]{2,1,0:T(8,128)S(1)}, f32[256,128]{1,0:T(8,128)S(1)}) custom-call(f32[8,64,4,1,128]{4,3,2,1,0:T(1,128)} %bitcast.7, f32[8,256,128]{2,1,0:T(8,128)} %bitcast.8, f32[2,64,4,1,128]{4,3,2,1,0:T(1,128)} %bitcast.9, f32[2,256,128]{2,1,0:T(8,128)} %bitcast.10, f32[4,128]{1,0:T(4,128)} %cosz_hbm.1, f32[4,128]{1,0:T(4,128)} %albedo_hbm.1, ...), custom_call_target="tpu_custom_call" | custom-call | tf_op jit(solution)/shard_map/advect_radiate/pallas_call | solution.py:590
  40.3 1.1 %store_results.1 = (f32[8,256,128]{2,1,0:T(8,128)}, f32[256,128]{1,0:T(8,128)}) custom-call(f32[8,256,128]{2,1,0:T(8,128)S(1)} %get-tuple-element.6.new_ref, f32[256,128]{1,0:T(8,128)S(1)} %get-tuple-element.7.heat_ref), custom_call_target="tpu_custom_call" | custom-call | tf_op jit(solution)/shard_map/store_results/pallas_call | solution.py:654

commit v2 on v1

--- a/solution.py
+++ b/solution.py
@@ -9,6 +9,7 @@
 
 MESH = pl.DeviceIdType.MESH
 HALO = 2
+EARLY = 4
 
 
 def step_kernel(
@@ -44,9 +45,15 @@
     rad_b,
     rad_c,
     rad_g,
-    pack_own,
-    pack_send,
-    pack_recv,
+    band,
+    c_edge,
+    pack_q,
+    pack_s,
+    edge_buf,
+    send_1,
+    recv_1,
+    send_2,
+    recv_2,
     own_sem,
     small_sem,
     go_sem,
@@ -56,8 +63,10 @@
     z2_recv,
     cn_send,
     cn_recv,
-    x_send,
-    x_recv,
+    x1_send,
+    x1_recv,
+    x2_send,
+    x2_recv,
 ):
     nf, lev, rows, lanes, bands, n_lat, n_lon = dims
     groups = lev // 8
@@ -202,22 +211,31 @@
         device_id_type=MESH,
     )
 
-    def x_copy(n, side):
+    def x1_copy(side):
         return pltpu.make_async_remote_copy(
-            src_ref=pack_send.at[side, n],
-            dst_ref=pack_recv.at[side, n],
-            send_sem=x_send.at[side, n],
-            recv_sem=x_recv.at[side, n],
+            src_ref=send_1.at[side],
+            dst_ref=recv_1.at[side],
+            send_sem=x1_send.at[side],
+            recv_sem=x1_recv.at[side],
             device_id=right_id if side == 0 else left_id,
             device_id_type=MESH,
         )
 
+    def x2_copy(n, side):
+        return pltpu.make_async_remote_copy(
+            src_ref=send_2.at[side, n],
+            dst_ref=recv_2.at[side, n],
+            send_sem=x2_send.at[side, n],
+            recv_sem=x2_recv.at[side, n],
+            device_id=right_id if side == 0 else left_id,
+            device_id_type=MESH,
+        )
+
     @pl.when(has_up)
     def _():
         cn_copy.start()
 
-    @pl.loop(0, nf)
-    def _(f):
+    def z1_start(f):
         @pl.when(has_up)
         def _():
             for r in range(HALO):
@@ -227,6 +245,12 @@
         def _():
             for r in range(HALO):
                 z1_copy(f, 1, r).start()
+
+    pl.loop(0, EARLY)(z1_start)
+
+    @pl.when(is_near)
+    def _():
+        pl.loop(EARLY, nf)(z1_start)
 
     zero = jnp.zeros((8, lanes), jnp.float32)
 
@@ -268,13 +292,13 @@
                 )
         return packed
 
-    def send_pair(n, even, odd):
-        pack_send[0, n] = jnp.where(own_half, even, pltpu.roll(odd, 2, 1))
-        pack_send[1, n] = jnp.where(own_half, pltpu.roll(even, lanes - 2, 1), odd)
-
-    def recv_pair(n, odd):
-        from_left = pack_recv[0, n]
-        from_right = pack_recv[1, n]
+    def send_pair(buf, n, even, odd):
+        buf[0, n] = jnp.where(own_half, even, pltpu.roll(odd, 2, 1))
+        buf[1, n] = jnp.where(own_half, pltpu.roll(even, lanes - 2, 1), odd)
+
+    def recv_pair(buf, n, odd):
+        from_left = buf[0, n]
+        from_right = buf[1, n]
         first = jnp.where(own_half, from_left, pltpu.roll(from_right, 2, 1))
         second = jnp.where(own_half, pltpu.roll(from_left, lanes - 2, 1), from_right)
         return jnp.where(odd, second, first)
@@ -282,26 +306,26 @@
     def own_row(f, r, g):
         return q_buf[f, pl.ds(8 * rows * g + r, 8, stride=rows), :]
 
+    def courant_row(n, r, g):
+        return c_buf[n, pl.ds(8 * rows * g + r, 8, stride=rows), :]
+
     @pl.loop(0, nf)
     def _(f):
         field_copy(f).wait()
-        pack_own[f] = pack(lambda r, g: own_row(f, r, g))
+        pack_q[f] = pack(lambda r, g: own_row(f, r, g))
 
     c_copy.wait()
     pairs_f = nf // 2
-    c_slot = 2 * pairs_f
-    c_pack = pack(lambda r, g: c_buf[0, pl.ds(8 * rows * g + r, 8, stride=rows), :])
+    c_pack = pack(lambda r, g: courant_row(0, r, g))
     for n in range(pairs_f):
-        send_pair(n, pack_own[2 * n], pack_own[2 * n + 1])
-    send_pair(c_slot, c_pack, c_pack)
-    first_slots = list(range(pairs_f)) + [c_slot]
-
-    def send_first(where, sides):
-        for side in sides:
-            @pl.when(where & jnp.logical_not(far_right if side == 0 else far_left))
-            def _():
-                for n in first_slots:
-                    x_copy(n, side).start()
+        send_pair(send_1, n, pack_q[2 * n], pack_q[2 * n + 1])
+    send_pair(send_1, pairs_f, c_pack, c_pack)
+    c_edge[0] = c_pack * (1.0 / 12.0)
+
+    for side in range(2):
+        @pl.when(jnp.logical_not(far_right if side == 0 else far_left))
+        def _():
+            x1_copy(side).start()
 
     def send_far(where):
         @pl.when(where & is_far)
@@ -311,11 +335,20 @@
         for side in range(2):
             @pl.when(where & (far_right if side == 0 else far_left))
             def _():
-                for n in first_slots:
-                    x_copy(n, side).start()
-
-    send_first(lon >= 0, (0, 1))
+                x1_copy(side).start()
+
+        @pl.when(where & is_far)
+        def _():
+            pl.loop(EARLY, nf)(z1_start)
+
     send_far(late_half)
+
+    ahead = lax.broadcasted_iota(jnp.int32, (2 * lanes, 2 * lanes), 0) & (lanes - 1)
+    column = lax.broadcasted_iota(jnp.int32, (2 * lanes, 2 * lanes), 1)
+    ahead = ahead - jnp.where(column < lanes, column, column - lanes - 1)
+    inner = (ahead == 0) | (ahead == 1)
+    outer = (ahead == -1) | (ahead == 2)
+    band[...] = jnp.where(inner, 7.0, jnp.where(outer, -1.0, 0.0)).astype(jnp.bfloat16)
 
     for copy in small:
         copy.wait()
@@ -413,54 +446,79 @@
     lax.fori_loop(0, lev // 2, down_pair, (start, net_flux(0, start)))
     send_far(early_half)
 
-    def x_wait(n):
-        x_copy(n, 0).wait_recv()
-        x_copy(n, 1).wait_recv()
-
-    x_wait(c_slot)
-
     @pl.when(has_dn)
     def _():
         cn_copy.wait_recv()
 
-    c_halo = recv_pair(c_slot, False)
     for r in range(rows):
         for g in range(groups):
-            k = r * groups + g
-            here = c_buf[0, pl.ds(8 * rows * g + r, 8, stride=rows), :]
-            edge = pltpu.roll(c_halo, (lanes - 2 - 4 * k) % lanes, 1)
-            west = pltpu.roll(jnp.where(lane == lanes - 1, edge, here), 1, 1)
-            c_west[r, pl.ds(8 * g, 8), :] = west * (1.0 / 12.0)
-            c_east[r, pl.ds(8 * g, 8), :] = here * (1.0 / 12.0)
-            north = c_buf[1, pl.ds(8 * rows * g + r, 8, stride=rows), :]
-            c_north[r + 1, pl.ds(8 * g, 8), :] = north * (1.0 / 12.0)
+            here = courant_row(0, r, g) * (1.0 / 12.0)
+            c_east[r, pl.ds(8 * g, 8), :] = here
+            c_west[r, pl.ds(8 * g, 8), :] = jnp.where(lane == 0, 0.0, pltpu.roll(here, 1, 1))
+            c_north[r + 1, pl.ds(8 * g, 8), :] = courant_row(1, r, g) * (1.0 / 12.0)
     for g in range(groups):
         c_north[0, pl.ds(8 * g, 8), :] = c_north[0, pl.ds(8 * g, 8), :] * (1.0 / 12.0)
 
-    first_lane = lane == 0
-    first_two = lane < 2
-    last_lane = lane == lanes - 1
-    last_two = lane >= lanes - 2
-
-    def tendency(load, halo, emit):
+    def tendency(load, emit):
+        x = jnp.concatenate(
+            [load(HALO + r, g) for r in range(rows) for g in range(groups)], axis=0
+        )
+        upper = x.astype(jnp.bfloat16)
+        lower = (x - upper.astype(jnp.float32)).astype(jnp.bfloat16)
+        flux = jnp.dot(
+            jnp.concatenate([upper, lower], axis=1),
+            band[...],
+            preferred_element_type=jnp.float32,
+        )
         for g in range(groups):
             at = pl.ds(8 * g, 8)
-            q = [load(j, g, at) for j in range(rows + 2 * HALO)]
+            q = [load(j, g) for j in range(rows + 2 * HALO)]
             north = [
                 c_north[j, at, :] * (7.0 * (q[j + 1] + q[j + 2]) - (q[j] + q[j + 3]))
                 for j in range(rows + 1)
             ]
             for r in range(rows):
                 k = r * groups + g
-                here = q[r + HALO]
-                edge = pltpu.roll(halo, (lanes - 2 - 4 * k) % lanes, 1)
-                r1 = pltpu.roll(jnp.where(first_lane, edge, here), lanes - 1, 1)
-                r2 = pltpu.roll(jnp.where(first_two, edge, here), lanes - 2, 1)
-                l1 = pltpu.roll(jnp.where(last_lane, edge, here), 1, 1)
-                l2 = pltpu.roll(jnp.where(last_two, edge, here), 2, 1)
-                east = c_east[r, at, :] * (7.0 * (here + r1) - (l1 + r2))
-                west = c_west[r, at, :] * (7.0 * (l1 + here) - (l2 + r1))
-                emit(r, g, here, -((east - west) + (north[r + 1] - north[r])))
+                east = c_east[r, at, :] * flux[8 * k : 8 * k + 8, :lanes]
+                west = c_west[r, at, :] * flux[8 * k : 8 * k + 8, lanes:]
+                emit(r, g, q[r + HALO], (north[r] - north[r + 1]) - (east - west))
+
+    corner = lane & 3
+
+    def edge(halo, own):
+        m1 = pltpu.roll(halo, 1, 1)
+        m2 = pltpu.roll(halo, 2, 1)
+        p1 = pltpu.roll(halo, lanes - 1, 1)
+        p2 = pltpu.roll(halo, lanes - 2, 1)
+        beside = pltpu.roll(own, lanes - 1, 1)
+        east = jnp.where(
+            corner == 0,
+            -p2,
+            jnp.where(corner == 1, 7.0 * p1 - p2, jnp.where(corner == 2, -m1, 0.0)),
+        )
+        west = jnp.where(
+            corner == 0,
+            0.0,
+            jnp.where(
+                corner == 1,
+                -p1,
+                jnp.where(corner == 2, 7.0 * (m1 + own) - (m2 + beside), -m2),
+            ),
+        )
+        return c_edge[1] * west - c_edge[0] * east
+
+    edge_lanes = (lane < 2) | (lane >= lanes - 2)
+
+    def spread(packed, k):
+        return jnp.where(edge_lanes, pltpu.roll(packed, (lanes - 2 - 4 * k) % lanes, 1), 0.0)
+
+    def x1_wait():
+        x1_copy(0).wait_recv()
+        x1_copy(1).wait_recv()
+        beyond = recv_pair(recv_1, pairs_f, False) * (1.0 / 12.0)
+        c_edge[1] = jnp.where(
+            corner == 2, pltpu.roll(beyond, 1, 1), pltpu.roll(c_edge[0], 1, 1)
+        )
 
     def z1_wait(f):
         @pl.when(has_dn)
@@ -473,48 +531,79 @@
             for r in range(HALO):
                 z1_copy(f, 1, r).wait_recv()
 
-    for n in range(pairs_f):
-        x_wait(n)
-
-    @pl.loop(0, pairs_f)
-    def _(n):
-        packed = []
-        for odd in range(2):
-            f = 2 * n + odd
-            z1_wait(f)
-
-            def emit(r, g, here, change):
-                s_buf[f, HALO + r, pl.ds(8 * g, 8), :] = here + change
-
-            def load(j, g, at):
-                if j < HALO:
-                    return q_halo[f, j, at, :]
-                if j < HALO + rows:
-                    return own_row(f, j - HALO, g)
-                return q_halo[f, j - rows, at, :]
-
-            tendency(load, recv_pair(n, odd == 1), emit)
-            packed.append(pack(lambda r, g: s_buf[f, HALO + r, pl.ds(8 * g, 8), :]))
-
-            @pl.when(has_up)
-            def _():
-                z2_copy(f, 0).start()
-
-            @pl.when(has_dn)
-            def _():
-                z2_copy(f, 1).start()
-
-        m = pairs_f + n
-        send_pair(m, packed[0], packed[1])
-        x_copy(m, 0).start()
-        x_copy(m, 1).start()
-
-    def final(f, halo, extra):
+    def add_edge(f):
+        change = edge(recv_pair(recv_1, f // 2, f % 2 == 1), pack_q[f])
+        edge_buf[f] = change
+        pack_s[f] = pack_s[f] + change
+
+        @pl.when(f % 2 == 1)
+        def _():
+            n = f // 2
+            send_pair(send_2, n, pack_s[f - 1], pack_s[f])
+            x2_copy(n, 0).start()
+            x2_copy(n, 1).start()
+
+    def finish_section(f):
+        change = edge_buf[f]
+        for r in range(rows):
+            for g in range(groups):
+                at = pl.ds(8 * g, 8)
+                s_buf[f, HALO + r, at, :] = s_buf[f, HALO + r, at, :] + spread(
+                    change, r * groups + g
+                )
+
+        @pl.when(has_up)
+        def _():
+            z2_copy(f, 0).start()
+
+        @pl.when(has_dn)
+        def _():
+            z2_copy(f, 1).start()
+
+    pl.when(is_near)(x1_wait)
+
+    @pl.loop(0, nf)
+    def _(f):
+        z1_wait(f)
+
+        def load(j, g):
+            at = pl.ds(8 * g, 8)
+            if j < HALO:
+                return q_halo[f, j, at, :]
+            if j < HALO + rows:
+                return own_row(f, j - HALO, g)
+            return q_halo[f, j - rows, at, :]
+
+        parts = [zero] * rows
+
         def emit(r, g, here, change):
-            value = 0.5 * ((own_row(f, r, g) + here) + change)
-            if extra:
-                value = value + 0.5 * heat_ref[pl.ds(8 * rows * g + r, 8, stride=rows), :]
-            out_ref[f, pl.ds(8 * rows * g + r, 8, stride=rows), :] = value
+            k = r * groups + g
+            value = here + change
+            s_buf[f, HALO + r, pl.ds(8 * g, 8), :] = value
+            parts[r] = jnp.where(slot == k, pltpu.roll(value, (4 * k + 2) % lanes, 1), parts[r])
+
+        tendency(load, emit)
+        pack_s[f] = sum(parts[1:], parts[0])
+
+        @pl.when(is_near)
+        def _():
+            add_edge(f)
+            finish_section(f)
+
+    @pl.when(is_far)
+    def _():
+        x1_wait()
+        pl.loop(0, nf)(add_edge)
+        pl.loop(0, nf)(finish_section)
+
+    @pl.loop(0, nf)
+    def _(f):
+        n = f // 2
+
+        @pl.when(f % 2 == 0)
+        def _():
+            x2_copy(n, 0).wait_recv()
+            x2_copy(n, 1).wait_recv()
 
         @pl.when(has_dn)
         def _():
@@ -524,20 +613,19 @@
         def _():
             z2_copy(f, 1).wait_recv()
 
-        tendency(lambda j, g, at: s_buf[f, j, at, :], halo, emit)
-
-    x_wait(pairs_f)
-    final(0, recv_pair(pairs_f, False), True)
-
-    @pl.loop(1, nf)
-    def _(f):
-        n = pairs_f + f // 2
-
-        @pl.when(f % 2 == 0)
-        def _():
-            x_wait(n)
-
-        final(f, recv_pair(n, f % 2 == 1), False)
+        beyond = edge(recv_pair(recv_2, n, f % 2 == 1), pack_s[f])
+
+        def emit(r, g, here, change):
+            total = (own_row(f, r, g) + here) + (change + spread(beyond, r * groups + g))
+            out_ref[f, pl.ds(8 * rows * g + r, 8, stride=rows), :] = 0.5 * total
+
+        tendency(lambda j, g: s_buf[f, j, pl.ds(8 * g, 8), :], emit)
+
+        @pl.when(f == 0)
+        def _():
+            for i in range(rows * groups):
+                at = pl.ds(8 * i, 8)
+                out_ref[0, at, :] = out_ref[0, at, :] + 0.5 * heat_ref[at, :]
 
     @pl.loop(0, nf)
     def _(f):
@@ -557,9 +645,10 @@
     def _():
         cn_copy.wait_send()
 
-    for n in range(2 * pairs_f + 1):
-        x_copy(n, 0).wait_send()
-        x_copy(n, 1).wait_send()
+    for side in range(2):
+        x1_copy(side).wait_send()
+        for n in range(pairs_f):
+            x2_copy(n, side).wait_send()
 
 
 def store_kernel(parts, new_ref, heat_ref, new_hbm, out_heat_hbm, sem):
@@ -582,7 +671,7 @@
     hbm_spec = pl.BlockSpec(memory_space=pltpu.HBM)
     vmem_spec = pl.BlockSpec(memory_space=pltpu.VMEM)
     rad = pltpu.VMEM((lev + 1, bands // 2, 8, lanes), f32)
-    packs = nf + 1
+    pairs_f = nf // 2
     results = (
         jax.ShapeDtypeStruct((nf, lev * rows, lanes), f32),
         jax.ShapeDtypeStruct((lev * rows, lanes), f32),
@@ -614,9 +703,15 @@
             rad,
             rad,
             rad,
+            pltpu.VMEM((2 * lanes, 2 * lanes), jnp.bfloat16),
+            pltpu.VMEM((2, 8, lanes), f32),
             pltpu.VMEM((nf, 8, lanes), f32),
-            pltpu.VMEM((2, packs, 8, lanes), f32),
-            pltpu.VMEM((2, packs, 8, lanes), f32),
+            pltpu.VMEM((nf, 8, lanes), f32),
+            pltpu.VMEM((nf, 8, lanes), f32),
+            pltpu.VMEM((2, pairs_f + 1, 8, lanes), f32),
+            pltpu.VMEM((2, pairs_f + 1, 8, lanes), f32),
+            pltpu.VMEM((2, pairs_f, 8, lanes), f32),
+            pltpu.VMEM((2, pairs_f, 8, lanes), f32),
             pltpu.SemaphoreType.DMA((nf + 1,)),
             pltpu.SemaphoreType.DMA((7,)),
             pltpu.SemaphoreType.REGULAR,
@@ -626,8 +721,10 @@
             pltpu.SemaphoreType.DMA((2, nf)),
             pltpu.SemaphoreType.DMA,
             pltpu.SemaphoreType.DMA,
-            pltpu.SemaphoreType.DMA((2, packs)),
-            pltpu.SemaphoreType.DMA((2, packs)),
+            pltpu.SemaphoreType.DMA((2,)),
+            pltpu.SemaphoreType.DMA((2,)),
+            pltpu.SemaphoreType.DMA((2, pairs_f)),
+            pltpu.SemaphoreType.DMA((2, pairs_f)),
         ],
         compiler_params=pltpu.CompilerParams(
             collective_id=0, has_side_effects=True, vmem_limit_bytes=48 * 1024 * 1024

time: 41.5 us -> 34.4 us (0.83)
  Pallas kernels: 40.7 us -> 33.6 us
    pallas_call x1, Pallas kernels: 39.6 us -> 32.6 us  [per_device(): pl.pallas_call(functools.partial(step_kernel, dims), out_shape=(pltpu.VME...]
where the time goes in v2:
time: 34.4 us; the launch traced here: 34.3 us
  Pallas kernels  33.6 us (98%)
  between operations  0.64 us (2%)
    pallas_call x1, Pallas kernels, per_device(): pl.pallas_call(functools.partial(step_kernel, dims), out_shape=(pltpu.VME...  32.6 us
    pallas_call x1, Pallas kernels, per_device(): pl.pallas_call(functools.partial(store_kernel, nf), out_shape=results, in...  1.08 us

profile of v2, /device:TPU:32, one launch (start us, length us, event | category | flops | bytes accessed | tf_op | source)
XLA Modules:
  0.0 34.3 jit_solution(8027182741235506812)
XLA Ops:
  0.6 32.6 %advect_radiate.1 = (f32[8,256,128]{2,1,0:T(8,128)S(1)}, f32[256,128]{1,0:T(8,128)S(1)}) custom-call(f32[8,64,4,1,128]{4,3,2,1,0:T(1,128)} %bitcast.7, f32[8,256,128]{2,1,0:T(8,128)} %bitcast.8, f32[2,64,4,1,128]{4,3,2,1,0:T(1,128)} %bitcast.9, f32[2,256,128]{2,1,0:T(8,128)} %bitcast.10, f32[4,128]{1,0:T(4,128)} %cosz_hbm.1, f32[4,128]{1,0:T(4,128)} %albedo_hbm.1, ...), custom_call_target="tpu_custom_call" | custom-call | tf_op jit(solution)/shard_map/advect_radiate/pallas_call | solution.py:679
  33.2 1.1 %store_results.1 = (f32[8,256,128]{2,1,0:T(8,128)}, f32[256,128]{1,0:T(8,128)}) custom-call(f32[8,256,128]{2,1,0:T(8,128)S(1)} %get-tuple-element.6.new_ref, f32[256,128]{1,0:T(8,128)S(1)} %get-tuple-element.7.heat_ref), custom_call_target="tpu_custom_call" | custom-call | tf_op jit(solution)/shard_map/store_results/pallas_call | solution.py:751

commit v3 on v2

--- a/solution.py
+++ b/solution.py
@@ -9,7 +9,8 @@
 
 MESH = pl.DeviceIdType.MESH
 HALO = 2
-EARLY = 4
+EARLY_FIRST = 4
+EARLY_SECOND = 2
 
 
 def step_kernel(
@@ -246,11 +247,8 @@
             for r in range(HALO):
                 z1_copy(f, 1, r).start()
 
-    pl.loop(0, EARLY)(z1_start)
-
-    @pl.when(is_near)
-    def _():
-        pl.loop(EARLY, nf)(z1_start)
+    early = jnp.where(is_near, nf, jnp.where(late_half, EARLY_SECOND, EARLY_FIRST))
+    pl.loop(0, early)(z1_start)
 
     zero = jnp.zeros((8, lanes), jnp.float32)
 
@@ -339,7 +337,7 @@
 
         @pl.when(where & is_far)
         def _():
-            pl.loop(EARLY, nf)(z1_start)
+            pl.loop(early, nf)(z1_start)
 
     send_far(late_half)
 
@@ -543,7 +541,7 @@
             x2_copy(n, 0).start()
             x2_copy(n, 1).start()
 
-    def finish_section(f):
+    def spread_edge(f):
         change = edge_buf[f]
         for r in range(rows):
             for g in range(groups):
@@ -552,6 +550,7 @@
                     change, r * groups + g
                 )
 
+    def z2_start(f):
         @pl.when(has_up)
         def _():
             z2_copy(f, 0).start()
@@ -561,6 +560,7 @@
             z2_copy(f, 1).start()
 
     pl.when(is_near)(x1_wait)
+    held = nf - 2
 
     @pl.loop(0, nf)
     def _(f):
@@ -588,22 +588,43 @@
         @pl.when(is_near)
         def _():
             add_edge(f)
-            finish_section(f)
+            spread_edge(f)
+            z2_start(f)
+
+        @pl.when(is_far & (f == held - 1))
+        def _():
+            x1_wait()
+            pl.loop(0, held)(add_edge)
+            pl.loop(0, held)(spread_edge)
+
+        @pl.when(is_far & (f >= held))
+        def _():
+            add_edge(f)
 
     @pl.when(is_far)
     def _():
-        x1_wait()
-        pl.loop(0, nf)(add_edge)
-        pl.loop(0, nf)(finish_section)
+        pl.loop(0, held)(z2_start)
+
+        @pl.loop(held, nf)
+        def _(f):
+            spread_edge(f)
+            z2_start(f)
+
+    def x2_wait(n):
+        x2_copy(n, 0).wait_recv()
+        x2_copy(n, 1).wait_recv()
+
+    def second_edge(f):
+        return edge(recv_pair(recv_2, f // 2, f % 2 == 1), pack_s[f])
+
+    def out_rows(r, g):
+        return pl.ds(8 * rows * g + r, 8, stride=rows)
 
     @pl.loop(0, nf)
     def _(f):
-        n = f // 2
-
         @pl.when(f % 2 == 0)
         def _():
-            x2_copy(n, 0).wait_recv()
-            x2_copy(n, 1).wait_recv()
+            x2_wait(f // 2)
 
         @pl.when(has_dn)
         def _():
@@ -613,11 +634,11 @@
         def _():
             z2_copy(f, 1).wait_recv()
 
-        beyond = edge(recv_pair(recv_2, n, f % 2 == 1), pack_s[f])
+        beyond = second_edge(f)
 
         def emit(r, g, here, change):
             total = (own_row(f, r, g) + here) + (change + spread(beyond, r * groups + g))
-            out_ref[f, pl.ds(8 * rows * g + r, 8, stride=rows), :] = 0.5 * total
+            out_ref[f, out_rows(r, g), :] = 0.5 * total
 
         tendency(lambda j, g: s_buf[f, j, pl.ds(8 * g, 8), :], emit)
 

time: 34.4 us -> 32.4 us (0.942)
  Pallas kernels: 33.6 us -> 31.6 us
    pallas_call x1, Pallas kernels: 32.6 us -> 30.6 us  [per_device(): pl.pallas_call(functools.partial(step_kernel, dims), out_shape=(pltpu.VME...]
where the time goes in v3:
time: 32.4 us; the launch traced here: 32.3 us
  Pallas kernels  31.6 us (98%)
  between operations  0.64 us (2%)
    pallas_call x1, Pallas kernels, per_device(): pl.pallas_call(functools.partial(step_kernel, dims), out_shape=(pltpu.VME...  30.6 us
    pallas_call x1, Pallas kernels, per_device(): pl.pallas_call(functools.partial(store_kernel, nf), out_shape=results, in...  1.08 us

profile of v3, /device:TPU:32, one launch (start us, length us, event | category | flops | bytes accessed | tf_op | source)
XLA Modules:
  0.0 32.3 jit_solution(14987083048149003372)
XLA Ops:
  0.6 30.6 %advect_radiate.1 = (f32[8,256,128]{2,1,0:T(8,128)S(1)}, f32[256,128]{1,0:T(8,128)S(1)}) custom-call(f32[8,64,4,1,128]{4,3,2,1,0:T(1,128)} %bitcast.7, f32[8,256,128]{2,1,0:T(8,128)} %bitcast.8, f32[2,64,4,1,128]{4,3,2,1,0:T(1,128)} %bitcast.9, f32[2,256,128]{2,1,0:T(8,128)} %bitcast.10, f32[4,128]{1,0:T(4,128)} %cosz_hbm.1, f32[4,128]{1,0:T(4,128)} %albedo_hbm.1, ...), custom_call_target="tpu_custom_call" | custom-call | tf_op jit(solution)/shard_map/advect_radiate/pallas_call | solution.py:700
  31.2 1.1 %store_results.1 = (f32[8,256,128]{2,1,0:T(8,128)}, f32[256,128]{1,0:T(8,128)}) custom-call(f32[8,256,128]{2,1,0:T(8,128)S(1)} %get-tuple-element.6.new_ref, f32[256,128]{1,0:T(8,128)S(1)} %get-tuple-element.7.heat_ref), custom_call_target="tpu_custom_call" | custom-call | tf_op jit(solution)/shard_map/store_results/pallas_call | solution.py:772

commit v4 on v3

--- a/solution.py
+++ b/solution.py
@@ -614,18 +614,22 @@
         x2_copy(n, 0).wait_recv()
         x2_copy(n, 1).wait_recv()
 
+    def z2_sent(f):
+        @pl.when(has_up)
+        def _():
+            z2_copy(f, 0).wait_send()
+
+        @pl.when(has_dn)
+        def _():
+            z2_copy(f, 1).wait_send()
+
     def second_edge(f):
         return edge(recv_pair(recv_2, f // 2, f % 2 == 1), pack_s[f])
 
     def out_rows(r, g):
         return pl.ds(8 * rows * g + r, 8, stride=rows)
 
-    @pl.loop(0, nf)
-    def _(f):
-        @pl.when(f % 2 == 0)
-        def _():
-            x2_wait(f // 2)
-
+    def z2_wait(f):
         @pl.when(has_dn)
         def _():
             z2_copy(f, 0).wait_recv()
@@ -634,13 +638,48 @@
         def _():
             z2_copy(f, 1).wait_recv()
 
+    def final(f, load):
         beyond = second_edge(f)
 
         def emit(r, g, here, change):
             total = (own_row(f, r, g) + here) + (change + spread(beyond, r * groups + g))
             out_ref[f, out_rows(r, g), :] = 0.5 * total
 
-        tendency(lambda j, g: s_buf[f, j, pl.ds(8 * g, 8), :], emit)
+        tendency(load, emit)
+
+    @pl.loop(0, nf)
+    def _(f):
+        @pl.when(has_up)
+        def _():
+            for r in range(HALO):
+                z1_copy(f, 0, r).wait_send()
+
+        @pl.when(has_dn)
+        def _():
+            for r in range(HALO):
+                z1_copy(f, 1, r).wait_send()
+
+    @pl.when(has_up)
+    def _():
+        cn_copy.wait_send()
+
+    for side in range(2):
+        x1_copy(side).wait_send()
+
+    @pl.loop(0, nf - 1)
+    def _(f):
+        @pl.when(f % 2 == 0)
+        def _():
+            x2_wait(f // 2)
+            x2_copy(f // 2, 0).wait_send()
+            x2_copy(f // 2, 1).wait_send()
+
+        @pl.when(f > 0)
+        def _():
+            z2_sent(f - 1)
+
+        z2_wait(f)
+        final(f, lambda j, g: s_buf[f, j, pl.ds(8 * g, 8), :])
 
         @pl.when(f == 0)
         def _():
@@ -648,28 +687,33 @@
                 at = pl.ds(8 * i, 8)
                 out_ref[0, at, :] = out_ref[0, at, :] + 0.5 * heat_ref[at, :]
 
-    @pl.loop(0, nf)
-    def _(f):
-        @pl.when(has_up)
-        def _():
-            for r in range(HALO):
-                z1_copy(f, 0, r).wait_send()
-            z2_copy(f, 0).wait_send()
-
-        @pl.when(has_dn)
-        def _():
-            for r in range(HALO):
-                z1_copy(f, 1, r).wait_send()
-            z2_copy(f, 1).wait_send()
-
-    @pl.when(has_up)
-    def _():
-        cn_copy.wait_send()
-
-    for side in range(2):
-        x1_copy(side).wait_send()
-        for n in range(pairs_f):
-            x2_copy(n, side).wait_send()
+    last = nf - 1
+
+    def inner_row(j, g):
+        if j < HALO or j >= HALO + rows:
+            return zero
+        return s_buf[last, j, pl.ds(8 * g, 8), :]
+
+    z2_sent(last - 1)
+    final(last, inner_row)
+    z2_wait(last)
+    top = HALO + rows
+    for g in range(groups):
+        at = pl.ds(8 * g, 8)
+        below = s_buf[last, HALO - 1, at, :]
+        above = s_buf[last, top, at, :]
+        low_face = c_north[0, at, :] * (7.0 * below - s_buf[last, HALO - 2, at, :])
+        high_face = c_north[rows, at, :] * (7.0 * above - s_buf[last, top + 1, at, :])
+        low_next = c_north[1, at, :] * below
+        high_next = c_north[rows - 1, at, :] * above
+        terms = {0: low_face + low_next, 1: -low_next}
+        for r, term in ((rows - 2, high_next), (rows - 1, -high_next - high_face)):
+            terms[r] = terms[r] + term if r in terms else term
+        for r in sorted(terms):
+            rows_at = out_rows(r, g)
+            out_ref[last, rows_at, :] = out_ref[last, rows_at, :] + 0.5 * terms[r]
+
+    z2_sent(last)
 
 
 def store_kernel(parts, new_ref, heat_ref, new_hbm, out_heat_hbm, sem):

time: 32.4 us -> 32.3 us (level)
  no operation moved by 1% of the time
where the time goes in v4:
time: 32.3 us; the launch traced here: 32.2 us
  Pallas kernels  31.5 us (98%)
  between operations  0.64 us (2%)
    pallas_call x1, Pallas kernels, per_device(): pl.pallas_call(functools.partial(step_kernel, dims), out_shape=(pltpu.VME...  30.5 us
    pallas_call x1, Pallas kernels, per_device(): pl.pallas_call(functools.partial(store_kernel, nf), out_shape=results, in...  1.08 us

profile of v4, /device:TPU:32, one launch (start us, length us, event | category | flops | bytes accessed | tf_op | source)
XLA Modules:
  0.0 32.2 jit_solution(9167567312807951064)
XLA Ops:
  0.6 30.5 %advect_radiate.1 = (f32[8,256,128]{2,1,0:T(8,128)S(1)}, f32[256,128]{1,0:T(8,128)S(1)}) custom-call(f32[8,64,4,1,128]{4,3,2,1,0:T(1,128)} %bitcast.7, f32[8,256,128]{2,1,0:T(8,128)} %bitcast.8, f32[2,64,4,1,128]{4,3,2,1,0:T(1,128)} %bitcast.9, f32[2,256,128]{2,1,0:T(8,128)} %bitcast.10, f32[4,128]{1,0:T(4,128)} %cosz_hbm.1, f32[4,128]{1,0:T(4,128)} %albedo_hbm.1, ...), custom_call_target="tpu_custom_call" | custom-call | tf_op jit(solution)/shard_map/advect_radiate/pallas_call | solution.py:744
  31.1 1.1 %store_results.1 = (f32[8,256,128]{2,1,0:T(8,128)}, f32[256,128]{1,0:T(8,128)}) custom-call(f32[8,256,128]{2,1,0:T(8,128)S(1)} %get-tuple-element.6.new_ref, f32[256,128]{1,0:T(8,128)S(1)} %get-tuple-element.7.heat_ref), custom_call_target="tpu_custom_call" | custom-call | tf_op jit(solution)/shard_map/store_results/pallas_call | solution.py:816

commit v5 on v4

--- a/solution.py
+++ b/solution.py
@@ -11,6 +11,7 @@
 HALO = 2
 EARLY_FIRST = 4
 EARLY_SECOND = 2
+YIELD = 3
 
 
 def step_kernel(
@@ -247,7 +248,8 @@
             for r in range(HALO):
                 z1_copy(f, 1, r).start()
 
-    early = jnp.where(is_near, nf, jnp.where(late_half, EARLY_SECOND, EARLY_FIRST))
+    early = jnp.where(is_partner & late_half, YIELD, nf)
+    early = jnp.where(is_near, early, jnp.where(late_half, EARLY_SECOND, EARLY_FIRST))
     pl.loop(0, early)(z1_start)
 
     zero = jnp.zeros((8, lanes), jnp.float32)
@@ -443,6 +445,11 @@
     start = tuple(zero for _ in range(pairs))
     lax.fori_loop(0, lev // 2, down_pair, (start, net_flux(0, start)))
     send_far(early_half)
+
+    @pl.when(is_partner)
+    def _():
+        pl.loop(early, nf)(z1_start)
+
 
     @pl.when(has_dn)
     def _():

time: 32.3 us -> 31.9 us (0.988)
  Pallas kernels: 31.5 us -> 31 us
    pallas_call x1, Pallas kernels: 30.5 us -> 29.9 us  [per_device(): pl.pallas_call(functools.partial(step_kernel, dims), out_shape=(pltpu.VME...]
where the time goes in v5:
time: 31.9 us; the launch traced here: 31.6 us
  Pallas kernels  31 us (97%)
  between operations  0.64 us (2%)
    pallas_call x1, Pallas kernels, per_device(): pl.pallas_call(functools.partial(step_kernel, dims), out_shape=(pltpu.VME...  29.9 us
    pallas_call x1, Pallas kernels, per_device(): pl.pallas_call(functools.partial(store_kernel, nf), out_shape=results, in...  1.08 us

profile of v5, /device:TPU:32, one launch (start us, length us, event | category | flops | bytes accessed | tf_op | source)
XLA Modules:
  0.0 31.6 jit_solution(4684492782702055367)
XLA Ops:
  0.6 29.9 %advect_radiate.1 = (f32[8,256,128]{2,1,0:T(8,128)S(1)}, f32[256,128]{1,0:T(8,128)S(1)}) custom-call(f32[8,64,4,1,128]{4,3,2,1,0:T(1,128)} %bitcast.7, f32[8,256,128]{2,1,0:T(8,128)} %bitcast.8, f32[2,64,4,1,128]{4,3,2,1,0:T(1,128)} %bitcast.9, f32[2,256,128]{2,1,0:T(8,128)} %bitcast.10, f32[4,128]{1,0:T(4,128)} %cosz_hbm.1, f32[4,128]{1,0:T(4,128)} %albedo_hbm.1, ...), custom_call_target="tpu_custom_call" | custom-call | tf_op jit(solution)/shard_map/advect_radiate/pallas_call | solution.py:751
  30.6 1.1 %store_results.1 = (f32[8,256,128]{2,1,0:T(8,128)}, f32[256,128]{1,0:T(8,128)}) custom-call(f32[8,256,128]{2,1,0:T(8,128)S(1)} %get-tuple-element.6.new_ref, f32[256,128]{1,0:T(8,128)S(1)} %get-tuple-element.7.heat_ref), custom_call_target="tpu_custom_call" | custom-call | tf_op jit(solution)/shard_map/store_results/pallas_call | solution.py:823
